TPU v7x, 256 devices: a whole 4x4x8 slice. The times are simulated.
256 devices in a mesh: ctx: 8 (over z), head: 32 (over y, x, core).
Axes of the slice: x: 4, y: 4, z: 8, core: 2. Of those that a mesh axis runs over, the one named last changes fastest.
Arguments:
- x_stream: bfloat16 [32768, 16384], P('ctx', 'head'), may hold values from -6 to 6
- gate_z: bfloat16 [32768, 16384], P('ctx', 'head'), as said below
- state_proj: bfloat16 [32768, 2048], P('ctx', 'head'), may hold values from -5 to 5
- dt_raw: float32 [32768, 256], P('ctx', 'head'), as said below
- dt_bias: float32 [256], P('head'), may hold values from -3 to -1
- a_log: float32 [256], P('head'), as said below
- skip_d: float32 [256], P('head'), may hold values from 0.5 to 1.5
- conv_x: bfloat16 [4, 16384], P(None, 'head'), may hold values from -3 to 3
- conv_proj: bfloat16 [4, 2048], P(None, 'head'), may hold values from -3 to 3
- norm_gain: float32 [16384], P('head'), may hold values from 0.5 to 1.5
Outputs:
- mixer_out: bfloat16 [32768, 16384], P('ctx', 'head')
Inputs may be any that keep to these rules, and one draw needn't show every extreme that they name: gate_z is a bounded normal draw whose scale varies by column. dt_raw is bounded; its level varies over blocks of 4096 tokens and heads. a_log is finite.
All inputs are finite; a program needn't handle non-finite values.
Results may differ from a plain program's by a relative error of at most 0.0085.
Values may be sent and summed in bfloat16 or wider, within the bound.
No kernel may reach another device: no remote copies, remote signals or barrier semaphores. Data moves between devices by JAX's collectives and lax.ppermute only.
A program may use at most 128 MiB of HBM per device.

v0:
```python
import jax
import jax.numpy as jnp
from jax import lax
from jax.sharding import PartitionSpec as P

HEADS = 256
STATE = 128
GROUPS = 8
BLOCK_LEN = 128


def passed_along(x, axis, by):
    count = lax.axis_size(axis)
    pairs = [(i, i + by) for i in range(count) if 0 <= i + by < count]
    return lax.ppermute(x, axis, pairs)


def swapped(value, axis, bit):
    mask = 2**bit
    pairs = [(source, source ^ mask) for source in range(lax.axis_size(axis))]
    return lax.ppermute(value, axis, pairs)


def conv_silu(sequence, edge_rows, weight):
    kernel_len = weight.shape[0]
    length = sequence.shape[0]
    padded = jnp.concatenate([edge_rows, sequence], axis=0).astype(jnp.float32)
    weight_wide = weight.astype(jnp.float32)
    total = jnp.zeros(sequence.shape, jnp.float32)
    for offset in range(kernel_len):
        total = total + weight_wide[offset] * padded[offset : offset + length]
    return jax.nn.silu(total).astype(jnp.bfloat16)


def join_pair(mine, other, upper):
    return jnp.where(
        upper, jnp.concatenate([other, mine], axis=1), jnp.concatenate([mine, other], axis=1)
    )


def block_scan(x_blocks, b_blocks, c_blocks, step_size, log_decay):
    highest = lax.Precision.HIGHEST
    running = jnp.cumsum(jnp.swapaxes(log_decay, 1, 2), axis=2)
    step_heads = jnp.swapaxes(step_size, 1, 2)
    gram_matrix = jnp.einsum("ctn,csn->cts", c_blocks, b_blocks, preferred_element_type=jnp.float32)
    block_len = running.shape[2]
    row_ids = jnp.arange(block_len)[:, None]
    col_ids = jnp.arange(block_len)[None, :]
    causal_mask = row_ids >= col_ids
    log_gaps = running[:, :, :, None] - running[:, :, None, :]
    decay_matrix = jnp.where(causal_mask, jnp.exp(jnp.where(causal_mask, log_gaps, 0.0)), 0.0)
    weights = (gram_matrix[:, None] * decay_matrix * step_heads[:, :, None, :]).astype(jnp.bfloat16)
    intra_out = jnp.einsum("chts,cshp->cthp", weights, x_blocks, preferred_element_type=jnp.float32)
    block_total = running[:, :, -1]
    state_weight = jnp.exp(block_total[:, :, None] - running) * step_heads
    weighted = (x_blocks.astype(jnp.float32) * jnp.swapaxes(state_weight, 1, 2)[..., None]).astype(
        jnp.bfloat16
    )
    states = jnp.einsum("cshp,csn->chpn", weighted, b_blocks, preferred_element_type=jnp.float32)

    def advance(state_now, inputs):
        factor, addend = inputs
        return (factor[:, None, None] * state_now + addend, state_now)

    empty_state = jnp.zeros(states.shape[1:], jnp.float32)
    final_state, entering = lax.scan(advance, empty_state, (jnp.exp(block_total), states))
    c_wide = c_blocks.astype(jnp.float32)
    inter_out = jnp.exp(jnp.swapaxes(running, 1, 2))[..., None] * jnp.einsum(
        "ctn,chpn->cthp", c_wide, entering, precision=highest
    )
    return (intra_out + inter_out, final_state, block_total, running)


def on_device(
    x_stream, gate_z, state_proj, dt_raw, dt_bias, a_log, skip_d, conv_x, conv_proj, norm_gain
):
    highest = lax.Precision.HIGHEST
    kernel_len = conv_x.shape[0]
    tokens_here = x_stream.shape[0]
    heads_here = dt_raw.shape[1]
    channels = x_stream.shape[1]
    head_size = channels // heads_here
    head_pos = lax.axis_index("head")
    group_devices = lax.axis_size("head") // GROUPS
    group_levels = group_devices.bit_length() - 1
    edge_start = tokens_here - kernel_len + 1
    edge_rows = passed_along((x_stream[edge_start:], state_proj[edge_start:]), "ctx", 1)
    x_conv = conv_silu(x_stream, edge_rows[0], conv_x)
    own_cols = conv_silu(state_proj, edge_rows[1], conv_proj)
    for level in range(group_levels):
        upper = head_pos >> level & 1 == 1
        other_cols = swapped(own_cols, "head", level)
        own_cols = join_pair(own_cols, other_cols, upper)
    blocks = tokens_here // BLOCK_LEN
    b_blocks = own_cols[:, :STATE].reshape(blocks, BLOCK_LEN, STATE)
    c_blocks = own_cols[:, STATE:].reshape(blocks, BLOCK_LEN, STATE)
    step_size = jax.nn.softplus(dt_raw + dt_bias)
    log_decay = step_size * -jnp.exp(a_log)
    local_out, final_state, block_total, running = block_scan(
        x_conv.reshape(blocks, BLOCK_LEN, heads_here, head_size),
        b_blocks,
        c_blocks,
        step_size.reshape(blocks, BLOCK_LEN, heads_here),
        log_decay.reshape(blocks, BLOCK_LEN, heads_here),
    )
    block_log = jnp.sum(block_total, axis=0)
    block_logs = lax.all_gather(block_log[None], "ctx", axis=0, tiled=True)
    ctx_pos = lax.axis_index("ctx")
    count = block_logs.shape[0]
    indices = jnp.arange(count)
    between = (indices[None, :] > indices[:, None]) & (indices[None, :] < ctx_pos)
    span_logs = jnp.dot(between.astype(jnp.float32), block_logs, precision=highest)
    weight_all = jnp.where(indices[:, None] < ctx_pos, jnp.exp(span_logs), 0.0)
    entering = jnp.zeros(final_state.shape, jnp.float32) + jnp.einsum(
        "rh,rhpn->hpn",
        weight_all,
        lax.all_gather(final_state[None].astype(jnp.bfloat16), "ctx", axis=0, tiled=True).astype(
            jnp.float32
        ),
        precision=highest,
    )
    block_start = jnp.cumsum(block_total, axis=0) - block_total
    carried_out = jnp.exp(jnp.swapaxes(running + block_start[:, :, None], 1, 2))[
        ..., None
    ] * jnp.einsum("ctn,hpn->cthp", c_blocks.astype(jnp.float32), entering, precision=highest)
    mixed = (local_out + carried_out).reshape(tokens_here, heads_here, head_size)
    mixed = mixed + skip_d[None, :, None] * x_conv.astype(jnp.float32).reshape(
        tokens_here, heads_here, head_size
    )
    gated_out = mixed.reshape(tokens_here, channels) * jax.nn.silu(gate_z.astype(jnp.float32))
    group_total = jnp.sum(gated_out * gated_out, axis=1)
    for level in range(group_levels):
        group_total = group_total + swapped(group_total, "head", level)
    mean_square = group_total / (HEADS // GROUPS * head_size)
    normed = gated_out * lax.rsqrt(mean_square + 1e-05)[:, None] * norm_gain[None, :]
    return normed.astype(jnp.bfloat16)


def solution(mesh):
    return jax.shard_map(
        on_device,
        mesh=mesh,
        in_specs=(
            P("ctx", "head"),
            P("ctx", "head"),
            P("ctx", "head"),
            P("ctx", "head"),
            P("head"),
            P("head"),
            P("head"),
            P(None, "head"),
            P(None, "head"),
            P("head"),
        ),
        out_specs=P("ctx", "head"),
        check_vma=False,
    )
```

profile of v0, /device:TPU:2, one launch (start us, length us, event | category | flops | bytes accessed | tf_op | source)
XLA Modules:
  0.0 275.4 jit_solution(6585836205751092210)
XLA Ops:
  7.5 3.8 %collective-permute-start.1 = (bf16[3,64]{0,1:T(8,128)(2,1)S(1)}, bf16[3,64]{0,1:T(8,128)(2,1)S(1)}, u32[]{:S(2)}, u32[]{:S(2)}) collective-permute-start(bf16[3,64]{0,1:T(8,128)(2,1)S(1)} %slice.73), channel_id=1, source_target_pairs={{0,32},{32,64},{64,96},{96,128},{128,160},{160,192},{192,224},{1,3... | collective-permute-start | bytes 1160 | tf_op jit(solution)/shard_map/ppermute | solution.py:15
  12.2 3.8 %collective-permute-start = (bf16[3,512]{0,1:T(8,128)(2,1)S(1)}, bf16[3,512]{0,1:T(8,128)(2,1)S(1)}, u32[]{:S(2)}, u32[]{:S(2)}) collective-permute-start(bf16[3,512]{0,1:T(8,128)(2,1)S(1)} %copy.30), channel_id=1, source_target_pairs={{0,32},{32,64},{64,96},{96,128},{128,160},{160,192},{192,224},{1,3... | collective-permute-start | bytes 9224 | tf_op jit(solution)/shard_map/ppermute | solution.py:15
  16.0 6.5 %copy.31 = bf16[4096,512]{0,1:T(8,128)(2,1)} copy(bf16[4096,512]{1,0:T(8,128)(2,1)} %param.12) | data formatting | bytes 8388608 | tf_op args[0]
  23.4 9.0 %reduce_window_sum.22 = f32[32,8,128]{2,1,0:T(8,128)S(1)} reduce-window(f32[32,8,128]{2,1,0:T(8,128)S(1)} %get-tuple-element.77, f32[]{:T(128)} %constant.42.clone.1), window={size=1x1x128 pad=0_0x0_0x127_0}, to_apply=%region_0.1 | reduce-window | flops 4161536 | bytes 262148 | tf_op jit(solution)/shard_map/jit(cumsum)/reduce_window_sum | solution.py:43
  35.5 17.0 %all-reduce = f32[64]{0:T(128)S(1)} all-reduce(f32[64]{0:T(128)S(1)} %dynamic-update-slice), channel_id=2, replica_groups=mesh['ctx'=8,'head'=32] {'ctx'}, use_global_device_ids=true, to_apply=%add | all-reduce | flops 64 | bytes 512
  55.1 6.3 %copy.43 = bf16[4096,512]{0,1:T(8,128)(2,1)} copy(bf16[4096,512]{1,0:T(8,128)(2,1)} %param.13) | data formatting | bytes 8388608 | tf_op args[1]
  64.3 2.5 maximum_convert_fusion
  67.8 8.7 %fusion.46 = bf16[64,8,32,128]{3,1,2,0:T(8,128)(2,1)} fusion(f32[4099,512]{0,1:T(8,128)S(1)} %maximum_convert_fusion, f32[512]{0:T(512)S(1)} %bitcast.109, f32[512]{0:T(512)S(1)} %bitcast.107, f32[512]{0:T(512)S(1)} %bitcast.105, f32[512]{0:T(512)S(1)} %bitcast.103), kind=kLoop, calls=%fused_computation.78 | loop fusion | flops 25165824 | bytes 37756928
  76.5 3.4 %copy.52 = bf16[64,8,32,128]{3,2,1,0:T(8,128)(2,1)S(1)} copy(bf16[64,8,32,128]{3,1,2,0:T(8,128)(2,1)} %fusion.46) | data formatting | bytes 8388608
  79.9 3.2 %multiply_convert_fusion.3 = bf16[32,128,8,64]{1,0,3,2:T(8,128)(2,1)} fusion(bf16[32,128,8,64]{1,0,3,2:T(8,128)(2,1)S(1)} %bitcast.95, f32[32,128,8]{1,0,2:T(8,128)S(1)} %copy.37), kind=kLoop, calls=%fused_computation.24 | loop fusion | flops 6291456 | bytes 8519680 | tf_op jit(solution)/shard_map/convert_element_type | solution.py:56
  83.2 8.8 %collective-permute-done.3 = bf16[4096,128]{0,1:T(8,128)(2,1)S(1)} collective-permute-done((bf16[4096,128]{0,1:T(8,128)(2,1)S(1)}, bf16[4096,128]{0,1:T(8,128)(2,1)S(1)}, u32[]{:S(2)}, u32[]{:S(2)}) %collective-permute-start.3) | collective-permute-done | bytes 1048608 | tf_op jit(solution)/shard_map/ppermute | solution.py:21
  93.3 7.6 %fusion.16 = f32[32,8,64,128]{3,2,1,0:T(8,128)} fusion(bf16[32,128,128,1]{2,1,3,0:T(8,128)(2,1)S(1)} %bitcast.97, bf16[32,128,8,64]{1,0,3,2:T(8,128)(2,1)} %multiply_convert_fusion.3), kind=kOutput, calls=%fused_computation.33 | convolution fusion | flops 536870912 | bytes 13631488 | tf_op jit(solution)/shard_map/cshp,csn->chpn/dot_general | solution.py:59
  100.9 79.2 %while.13 = (s32[]{:T(128)}, f32[8,64,128]{2,1,0:T(8,128)S(1)}, f32[32,8,64,128]{3,2,1,0:T(8,128)}, f32[32,8]{1,0:T(8,128)}, f32[32,8,64,128]{3,2,1,0:T(8,128)}, /*index=5*/s32[]{:T(128)}, s32[]{:T(128)}) while((s32[]{:T(128)}, f32[8,64,128]{2,1,0:T(8,128)S(1)}, f32[32,8,64,128]{3,2,1,0:T(8,128)}, f32[32,8]{1,0:T(8,128)}, ...), condition=%wide.region_2.3_spmd.clone, body=%wide.region_1.2_spmd.clone.sunk | while | flops 262147 | bytes 1311424 | solution.py:66
  102.3 1.0 bitcast_add_fusion.4
  104.8 1.0 bitcast_add_fusion.4
  107.2 1.0 bitcast_add_fusion.4
  109.7 1.0 bitcast_add_fusion.4
  114.7 1.0 bitcast_add_fusion.4
  117.1 1.0 bitcast_add_fusion.4
  119.6 1.0 bitcast_add_fusion.4
  122.1 1.0 bitcast_add_fusion.4
  132.0 1.0 bitcast_add_fusion.4
  134.5 1.0 bitcast_add_fusion.4
  137.0 1.0 bitcast_add_fusion.4
  139.4 1.0 bitcast_add_fusion.4
  141.9 1.0 bitcast_add_fusion.4
  144.4 1.0 bitcast_add_fusion.4
  151.8 1.0 bitcast_add_fusion.4
  154.3 1.0 bitcast_add_fusion.4
  156.7 1.0 bitcast_add_fusion.4
  159.2 1.0 bitcast_add_fusion.4
  161.7 1.0 bitcast_add_fusion.4
  164.1 1.0 bitcast_add_fusion.4
  166.6 1.0 bitcast_add_fusion.4
  174.0 1.0 bitcast_add_fusion.4
  176.5 1.0 bitcast_add_fusion.4
  179.0 1.0 bitcast_add_fusion.4
  182.3 8.4 %fusion.36 = f32[32,128,8,64]{1,3,2,0:T(8,128)} fusion(bf16[32,128,128,1]{2,1,3,0:T(8,128)(2,1)S(1)} %bitcast.93, f32[32,8,64,128]{3,2,1,0:T(8,128)} %get-tuple-element.33), kind=kOutput, calls=%fused_computation.77 | convolution fusion | flops 3221225472 | bytes 17825792 | tf_op jit(solution)/shard_map/ctn,chpn->cthp/dot_general | solution.py:68
  190.7 10.7 %fusion.1 = f32[32,8,64,128]{3,2,1,0:T(8,128)} fusion(f32[32,8,128]{2,1,0:T(8,128)S(1)} %copy-done.9, f32[32,8,128]{2,1,0:T(8,128)S(1)} %reduce_window_sum.22, f32[32,128,128]{2,1,0:T(8,128)S(1)} %fusion.35, pred[128,128]{1,0:T(8,128)(4,1)S(1)} %copy-done.11, bf16[32,128,8,64]{1,0,3,2:T(8,128)(2,1)S(1)} %bitcast.96), kind=kOutput, calls=%fused_computation.7 | convolution fusion | flops 562036736 | bytes 14958592 | tf_op jit(solution)/shard_map/chts,cshp->cthp/dot_general | solution.py:53
  201.4 19.5 %all-gather.4.cloned.1.call-done = bf16[64,64,128]{2,1,0:T(8,128)(2,1)} async-done(((bf16[8,64,128]{2,1,0:T(8,128)(2,1)}), bf16[64,64,128]{2,1,0:T(8,128)(2,1)}) %all-gather.4.cloned.1.call-update) | async-done | bytes 1048592 | tf_op jit(solution)/shard_map/all_gather | solution.py:117
  220.9 2.5 fusion.24
  223.5 8.3 %fusion.9 = f32[32,128,8,64]{1,3,2,0:T(8,128)S(1)} fusion(f32[32,8,64,128]{3,2,1,0:T(8,128)} %fusion.1, f32[32,128,8,64]{1,3,2,0:T(8,128)} %fusion.36, f32[32,128,8]{1,2,0:T(8,128)S(1)} %copy-done.7, f32[32,128,8]{1,2,0:T(8,128)S(1)} %copy-done.6, bf16[32,128,128,1]{2,1,3,0:T(8,128)(2,1)S(1)} %bitcast.94, f32[8,64,128,1]{2,1,0,3:T(8,128)S(1)} %bitcast.99), kind=kOutput, calls=%fused_computation.21 | convolution fusion | flops 3229614080 | bytes 26738688 | tf_op jit(solution)/shard_map/ctn,hpn->cthp/dot_general | solution.py:125
  231.8 8.0 %copy.42 = f32[32,128,8,64]{1,0,3,2:T(8,128)} copy(f32[32,128,8,64]{1,3,2,0:T(8,128)S(1)} %fusion.9) | data formatting | bytes 16777216 | tf_op jit(solution)/shard_map/add | solution.py:126
  239.9 13.9 %multiply_reduce_fusion = (f32[4096]{0:T(1024)S(1)}, f32[4096,512]{0,1:T(8,128)S(1)}) fusion(bf16[4096,512]{0,1:T(8,128)(2,1)S(1)} %copy-done.4, f32[512]{0:T(512)S(1)} %copy-done.13, f32[64,8,32,128]{3,2,1,0:T(8,128)} %bitcast.91, f32[4099,512]{0,1:T(8,128)S(1)} %bitcast.90, f32[512]{0:T(512)S(1)} %bitcast.110, f32[512]{0:T(512)S(1)} %bitcast.108, ...), kind=kLoop, calls=%fused_computation.23 | loop fusion | flops 48230400 | bytes 54552576 | tf_op jit(solution)/shard_map/reduce_sum | solution.py:131
  253.9 1.2 collective-permute-done.4
  255.5 3.2 %collective-permute-done.5 = f32[4096]{0:T(1024)S(1)} collective-permute-done((f32[4096]{0:T(1024)S(1)}, f32[4096]{0:T(1024)S(1)}, u32[]{:S(2)}, u32[]{:S(2)}) %collective-permute-start.5) | collective-permute-done | bytes 16416 | tf_op jit(solution)/shard_map/ppermute | solution.py:21
  258.8 3.3 %multiply_convert_fusion.2 = bf16[4096,512]{0,1:T(8,128)(2,1)} fusion(f32[4096,512]{0,1:T(8,128)S(1)} %get-tuple-element.74, f32[512]{0:T(512)S(1)} %copy-done.15, f32[4096]{0:T(1024)S(1)} %add_rsqrt_fusion), kind=kLoop, calls=%fused_computation.22 | loop fusion | flops 6291456 | bytes 12601344 | tf_op jit(solution)/shard_map/convert_element_type | solution.py:136
  262.2 6.4 %copy.44 = bf16[4096,512]{1,0:T(8,128)(2,1)} copy(bf16[4096,512]{0,1:T(8,128)(2,1)} %multiply_convert_fusion.2) | data formatting | bytes 8388608 | tf_op jit(solution)/shard_map/convert_element_type | solution.py:136
  (169 shorter events, 69.1 us)
Async XLA Ops:
  6.5 27.5 %copy-start.19 = (u32[256]{0:T(256)S(1)}, u32[256]{0:T(256)}, u32[]{:S(2)}) copy-start(u32[256]{0:T(256)} %constant.53) | copy-start | bytes 3076
  6.5 16.0 %copy-start.18 = (f32[8]{0:T(128)S(1)}, f32[8]{0:T(128)}, u32[]{:S(2)}) copy-start(f32[8]{0:T(128)} %param.17) | copy-start | bytes 100
  6.5 16.0 %copy-start.8 = (f32[4096,8]{0,1:T(8,128)S(1)}, f32[4096,8]{0,1:T(8,128)}, u32[]{:S(2)}) copy-start(f32[4096,8]{0,1:T(8,128)} %param.15) | copy-start | bytes 393220
  6.5 16.0 %copy-start.14 = (f32[8]{0:T(128)S(1)}, f32[8]{0:T(128)}, u32[]{:S(2)}) copy-start(f32[8]{0:T(128)} %param.16) | copy-start | bytes 100
  6.5 27.2 %copy-start.16 = (bf16[4,64]{1,0:T(4,128)(2,1)S(1)}, bf16[4,64]{1,0:T(4,128)(2,1)}, u32[]{:S(2)}) copy-start(bf16[4,64]{1,0:T(4,128)(2,1)} %param.20) | copy-start | bytes 1540
  6.5 27.2 %copy-start.12 = (bf16[4,512]{1,0:T(4,128)(2,1)S(1)}, bf16[4,512]{1,0:T(4,128)(2,1)}, u32[]{:S(2)}) copy-start(bf16[4,512]{1,0:T(4,128)(2,1)} %param.19) | copy-start | bytes 12292
  6.6 214.3 %all-gather.4.cloned.1.call-start = ((), (), s32[]{:S(2)}) async-start(), calls=%async_computation | async-start | bytes 1179648 | tf_op jit(solution)/shard_map/all_gather | solution.py:117
  7.5 54.6 %collective-permute-start.1 = (bf16[3,64]{0,1:T(8,128)(2,1)S(1)}, bf16[3,64]{0,1:T(8,128)(2,1)S(1)}, u32[]{:S(2)}, u32[]{:S(2)}) collective-permute-start(bf16[3,64]{0,1:T(8,128)(2,1)S(1)} %slice.73), channel_id=1, source_target_pairs={{0,32},{32,64},{64,96},{96,128},{128,160},{160,192},{192,224},{1,3... | collective-permute-start | bytes 1160 | tf_op jit(solution)/shard_map/ppermute | solution.py:15
  12.2 51.2 %collective-permute-start = (bf16[3,512]{0,1:T(8,128)(2,1)S(1)}, bf16[3,512]{0,1:T(8,128)(2,1)S(1)}, u32[]{:S(2)}, u32[]{:S(2)}) collective-permute-start(bf16[3,512]{0,1:T(8,128)(2,1)S(1)} %copy.30), channel_id=1, source_target_pairs={{0,32},{32,64},{64,96},{96,128},{128,160},{160,192},{192,224},{1,3... | collective-permute-start | bytes 9224 | tf_op jit(solution)/shard_map/ppermute | solution.py:15
  16.0 45.4 %copy-start.17 = (f32[8]{0:T(128)S(1)}, f32[8]{0:T(128)}, u32[]{:S(2)}) copy-start(f32[8]{0:T(128)} %param.18) | copy-start | bytes 100
  16.0 46.1 %copy-start.5 = (bf16[4096,64]{0,1:T(8,128)(2,1)S(1)}, bf16[4096,64]{0,1:T(8,128)(2,1)}, u32[]{:S(2)}) copy-start(bf16[4096,64]{0,1:T(8,128)(2,1)} %param.14) | copy-start | bytes 1572868
  62.1 2.2 copy-start.1
  63.2 3.5 %collective-permute-start.2 = (bf16[4096,64]{0,1:T(8,128)(2,1)S(1)}, bf16[4096,64]{0,1:T(8,128)(2,1)S(1)}, u32[]{:S(2)}, u32[]{:S(2)}) collective-permute-start(bf16[4096,64]{0,1:T(8,128)(2,1)S(1)} %multiply_convert_fusion.5), channel_id=1, source_target_pairs={{0,1},{1,0},{2,3},{3,2},{4,5},{5,4},{6,7},{7,6},{8,9},{9,8},{10,11... | collective-permute-start | bytes 1572872 | tf_op jit(solution)/shard_map/ppermute | solution.py:21
  66.8 9.7 %copy-start = (f32[4099,512]{0,1:T(8,128)}, f32[4099,512]{0,1:T(8,128)S(1)}, u32[]{:S(2)}) copy-start(f32[4099,512]{0,1:T(8,128)S(1)} %maximum_convert_fusion) | copy-start | bytes 25184260
  67.0 24.9 %collective-permute-start.3 = (bf16[4096,128]{0,1:T(8,128)(2,1)S(1)}, bf16[4096,128]{0,1:T(8,128)(2,1)S(1)}, u32[]{:S(2)}, u32[]{:S(2)}) collective-permute-start(bf16[4096,128]{0,1:T(8,128)(2,1)S(1)} %maximum_select_fusion.1), channel_id=1, source_target_pairs={{0,2},{1,3},{2,0},{3,1},{4,6},{5,7},{6,4},{7,5},{8,10},{9,11},{10,... | collective-permute-start | bytes 3145736 | tf_op jit(solution)/shard_map/ppermute | solution.py:21
  79.9 12.7 %copy-start.2 = (bf16[64,8,32,128]{3,2,1,0:T(8,128)(2,1)}, bf16[64,8,32,128]{3,2,1,0:T(8,128)(2,1)S(1)}, u32[]{:S(2)}) copy-start(bf16[64,8,32,128]{3,2,1,0:T(8,128)(2,1)S(1)} %copy.52) | copy-start | bytes 12582916
  182.3 8.4 %copy-start.3 = (bf16[64,8,32,128]{3,2,1,0:T(8,128)(2,1)S(1)}, bf16[64,8,32,128]{3,2,1,0:T(8,128)(2,1)}, u32[]{:S(2)}) copy-start(bf16[64,8,32,128]{3,2,1,0:T(8,128)(2,1)} %copy-done.2) | copy-start | bytes 12582916
  182.3 8.4 %copy-start.9 = (f32[32,8,128]{2,1,0:T(8,128)S(1)}, f32[32,8,128]{2,1,0:T(8,128)}, u32[]{:S(2)}) copy-start(f32[32,8,128]{2,1,0:T(8,128)} %get-tuple-element.78) | copy-start | bytes 393220
  182.3 8.4 %copy-start.11 = (pred[128,128]{1,0:T(8,128)(4,1)S(1)}, pred[128,128]{1,0:T(8,128)(4,1)}, u32[]{:S(2)}) copy-start(pred[128,128]{1,0:T(8,128)(4,1)} %iota_compare_fusion) | copy-start | bytes 49156
  190.7 30.2 %copy-start.10 = (f32[8,8,1,1]{0,2,3,1:T(1,128)S(1)}, f32[8,8,1,1]{0,2,3,1:T(1,128)}, u32[]{:S(2)}) copy-start(f32[8,8,1,1]{0,2,3,1:T(1,128)} %copy.47) | copy-start | bytes 772
  190.7 32.7 %copy-start.6 = (f32[32,128,8]{1,2,0:T(8,128)S(1)}, f32[32,128,8]{1,2,0:T(8,128)}, u32[]{:S(2)}) copy-start(f32[32,128,8]{1,2,0:T(8,128)} %get-tuple-element.81) | copy-start | bytes 393220
  190.7 32.7 %copy-start.7 = (f32[32,128,8]{1,2,0:T(8,128)S(1)}, f32[32,128,8]{1,2,0:T(8,128)}, u32[]{:S(2)}) copy-start(f32[32,128,8]{1,2,0:T(8,128)} %get-tuple-element.82) | copy-start | bytes 393220
  223.4 16.4 %slice-start = ((s8[8650752]{0:T(1024)(128)(4,1)}), s8[4194304]{0:T(1024)(128)(4,1)S(1)}, s32[]{:S(2)}) async-start(s8[8650752]{0:T(1024)(128)(4,1)} %bitcast.89), calls=%async_computation.1 | async-start | bytes 8388608
  223.4 16.4 %slice-start.1 = ((s8[8650752]{0:T(1024)(128)(4,1)}), s8[4194304]{0:T(1024)(128)(4,1)S(1)}, s32[]{:S(2)}) async-start(s8[8650752]{0:T(1024)(128)(4,1)} %bitcast.89), calls=%async_computation.2 | async-start | bytes 8388608
  231.8 8.1 %slice-start.2 = ((s8[8650752]{0:T(1024)(128)(4,1)}), s8[262144]{0:T(1024)(128)(4,1)S(1)}, s32[]{:S(2)}) async-start(s8[8650752]{0:T(1024)(128)(4,1)} %bitcast.89), calls=%async_computation.3 | async-start | bytes 524288
  231.8 8.1 %copy-start.4 = (bf16[4096,512]{0,1:T(8,128)(2,1)S(1)}, bf16[4096,512]{0,1:T(8,128)(2,1)}, u32[]{:S(2)}) copy-start(bf16[4096,512]{0,1:T(8,128)(2,1)} %copy.43) | copy-start | bytes 12582916
  231.8 8.0 %copy-start.13 = (f32[512]{0:T(512)S(1)}, f32[512]{0:T(512)}, u32[]{:S(2)}) copy-start(f32[512]{0:T(512)} %mul.228) | copy-start | bytes 6148
  239.9 18.9 %copy-start.15 = (f32[512]{0:T(512)S(1)}, f32[512]{0:T(512)}, u32[]{:S(2)}) copy-start(f32[512]{0:T(512)} %param.21) | copy-start | bytes 6148
  253.8 1.3 collective-permute-start.4
  255.1 3.7 %collective-permute-start.5 = (f32[4096]{0:T(1024)S(1)}, f32[4096]{0:T(1024)S(1)}, u32[]{:S(2)}, u32[]{:S(2)}) collective-permute-start(f32[4096]{0:T(1024)S(1)} %add.99), channel_id=1, source_target_pairs={{0,2},{1,3},{2,0},{3,1},{4,6},{5,7},{6,4},{7,5},{8,10},{9,11},{10,... | collective-permute-start | bytes 49160 | tf_op jit(solution)/shard_map/ppermute | solution.py:21
Sparse Core Ops, SparseCore 0:
  181.6 39.3 all-gather.3
where the time goes:
time: 278 us; the launch traced here: 275 us
  other arithmetic  103 us (37%)
  local copies, waits for them, and re-layouts  60.3 us (22%)
  matrix products  38.5 us (14%)
  waiting for transfers between devices  32.7 us (12%)
  blocking collectives  17 us (6%)
  between operations  14.5 us (5%)
  starting transfers between devices  9.16 us (3%)
    add x32, other arithmetic, advance(): return (factor[:, None, None] * state_now + addend, state_now)  33.3 us
    dynamic_update_slice x32, other arithmetic, block_scan(): lax.scan(advance, empty_state, (jnp.exp(block_total), states))  23.4 us
    mul x32, local copies, waits for them, and re-layouts, advance(): return (factor[:, None, None] * state_now + addend, state_now)  21.8 us
    all_gather x1, waiting for transfers between devices, on_device(): lax.all_gather(final_state[None].astype(jnp.bfloat16), 'ctx', axis=0, til...  19.5 us
    unnamed x53, local copies, waits for them, and re-layouts  18.7 us
    unnamed x1, blocking collectives  17 us
    reduce_sum x1, other arithmetic, on_device(): group_total = jnp.sum(gated_out * gated_out, axis=1)  13.9 us
    ppermute x4, waiting for transfers between devices, swapped(): return lax.ppermute(value, axis, pairs)  13.2 us
  transfers between devices with their start and end apart: 7, of which 4 were waited for; matrix products, arithmetic and copies ran while one was open for 25% of the time, Pallas kernels for 0%

commit v1 on v0

--- a/solution.py
+++ b/solution.py
@@ -74,6 +74,15 @@
 def on_device(
     x_stream, gate_z, state_proj, dt_raw, dt_bias, a_log, skip_d, conv_x, conv_proj, norm_gain
 ):
+
+    def region_apply(mine_x, net_axis, axis_k):
+        return jnp.concatenate(
+            lax.all_to_all(
+                jnp.stack([mine_x for _ in range(lax.axis_size(net_axis))]), net_axis, 0, 0
+            ),
+            axis=axis_k,
+        )
+
     highest = lax.Precision.HIGHEST
     kernel_len = conv_x.shape[0]
     tokens_here = x_stream.shape[0]
@@ -114,9 +123,7 @@
     entering = jnp.zeros(final_state.shape, jnp.float32) + jnp.einsum(
         "rh,rhpn->hpn",
         weight_all,
-        lax.all_gather(final_state[None].astype(jnp.bfloat16), "ctx", axis=0, tiled=True).astype(
-            jnp.float32
-        ),
+        region_apply(final_state[None].astype(jnp.bfloat16), "ctx", 0).astype(jnp.float32),
         precision=highest,
     )
     block_start = jnp.cumsum(block_total, axis=0) - block_total

time: 278 us -> 258 us (0.928)
  between operations: 14.5 us -> 1.17 us
  waiting for transfers between devices: 32.7 us -> 20.8 us
  starting transfers between devices: 9.16 us -> 15.2 us
    all_gather x1 -> x0, waiting for transfers between devices: 19.5 us -> none  [on_device(): lax.all_gather(final_state[None].astype(jnp.bfloat16), 'ctx', axis=0, til...]
    all_to_all x0 -> x1, waiting for transfers between devices: none -> 7.62 us  [region_apply(): lax.all_to_all(jnp.stack([mine_x for _ in range(lax.axis_size(net_axis))]...]
    all_to_all x0 -> x1, starting transfers between devices: none -> 6.04 us  [region_apply(): lax.all_to_all(jnp.stack([mine_x for _ in range(lax.axis_size(net_axis))]...]
  transfers between devices with their start and end apart: 7 -> 7, of which waited for: 4 -> 4; matrix products, arithmetic and copies ran while one was open for 25% -> 27% of each run, Pallas kernels for 0% -> 0%
where the time goes in v1:
time: 258 us; the launch traced here: 256 us
  other arithmetic  102 us (40%)
  local copies, waits for them, and re-layouts  61.5 us (24%)
  matrix products  37.2 us (14%)
  waiting for transfers between devices  20.8 us (8%)
  blocking collectives  17 us (7%)
  starting transfers between devices  15.2 us (6%)
    add x32, other arithmetic, advance(): return (factor[:, None, None] * state_now + addend, state_now)  33.3 us
    dynamic_update_slice x32, other arithmetic, block_scan(): lax.scan(advance, empty_state, (jnp.exp(block_total), states))  23.2 us
    mul x32, local copies, waits for them, and re-layouts, advance(): return (factor[:, None, None] * state_now + addend, state_now)  21.8 us
    unnamed x53, local copies, waits for them, and re-layouts  18.7 us
    unnamed x1, blocking collectives  17 us
    reduce_sum x1, other arithmetic, on_device(): group_total = jnp.sum(gated_out * gated_out, axis=1)  14.2 us
    ppermute x4, waiting for transfers between devices, swapped(): return lax.ppermute(value, axis, pairs)  13.1 us
    dot_general x1, matrix products, block_scan(): jnp.einsum('chts,cshp->cthp', weights, x_blocks, preferred_element_type=j...  10.7 us
  transfers between devices with their start and end apart: 7, of which 4 were waited for; matrix products, arithmetic and copies ran while one was open for 27% of the time, Pallas kernels for 0%

profile of v1, /device:TPU:2, one launch (start us, length us, event | category | flops | bytes accessed | tf_op | source)
XLA Modules:
  0.0 255.6 jit_solution(7766891509395893741)
XLA Ops:
  0.9 3.8 %collective-permute-start.1 = (bf16[3,64]{0,1:T(8,128)(2,1)S(1)}, bf16[3,64]{0,1:T(8,128)(2,1)S(1)}, u32[]{:S(2)}, u32[]{:S(2)}) collective-permute-start(bf16[3,64]{0,1:T(8,128)(2,1)S(1)} %slice.73), channel_id=1, source_target_pairs={{0,32},{32,64},{64,96},{96,128},{128,160},{160,192},{192,224},{1,3... | collective-permute-start | bytes 1160 | tf_op jit(solution)/shard_map/ppermute | solution.py:15
  5.6 3.8 %collective-permute-start = (bf16[3,512]{0,1:T(8,128)(2,1)S(1)}, bf16[3,512]{0,1:T(8,128)(2,1)S(1)}, u32[]{:S(2)}, u32[]{:S(2)}) collective-permute-start(bf16[3,512]{0,1:T(8,128)(2,1)S(1)} %copy.15), channel_id=1, source_target_pairs={{0,32},{32,64},{64,96},{96,128},{128,160},{160,192},{192,224},{1,3... | collective-permute-start | bytes 9224 | tf_op jit(solution)/shard_map/ppermute | solution.py:15
  9.5 6.5 %copy.16 = bf16[4096,512]{0,1:T(8,128)(2,1)} copy(bf16[4096,512]{1,0:T(8,128)(2,1)} %param.12) | data formatting | bytes 8388608 | tf_op args[0]
  16.8 9.0 %reduce_window_sum.22 = f32[32,8,128]{2,1,0:T(8,128)S(1)} reduce-window(f32[32,8,128]{2,1,0:T(8,128)S(1)} %get-tuple-element.72, f32[]{:T(128)} %constant.42.clone.1), window={size=1x1x128 pad=0_0x0_0x127_0}, to_apply=%region_0.1 | reduce-window | flops 4161536 | bytes 262148 | tf_op jit(solution)/shard_map/jit(cumsum)/reduce_window_sum | solution.py:43
  29.0 17.0 %all-reduce = f32[64]{0:T(128)S(1)} all-reduce(f32[64]{0:T(128)S(1)} %dynamic-update-slice), channel_id=2, replica_groups=mesh['ctx'=8,'head'=32] {'ctx'}, use_global_device_ids=true, to_apply=%add | all-reduce | flops 64 | bytes 512
  48.5 6.3 %copy.28 = bf16[4096,512]{0,1:T(8,128)(2,1)} copy(bf16[4096,512]{1,0:T(8,128)(2,1)} %param.13) | data formatting | bytes 8388608 | tf_op args[1]
  57.7 2.5 maximum_convert_fusion
  61.3 8.7 %fusion.46 = bf16[64,8,32,128]{3,1,2,0:T(8,128)(2,1)} fusion(f32[4099,512]{0,1:T(8,128)S(1)} %maximum_convert_fusion, f32[512]{0:T(512)S(1)} %bitcast.109, f32[512]{0:T(512)S(1)} %bitcast.107, f32[512]{0:T(512)S(1)} %bitcast.105, f32[512]{0:T(512)S(1)} %bitcast.103), kind=kLoop, calls=%fused_computation.78 | loop fusion | flops 25165824 | bytes 37756928
  69.9 3.4 %copy.37 = bf16[64,8,32,128]{3,2,1,0:T(8,128)(2,1)S(1)} copy(bf16[64,8,32,128]{3,1,2,0:T(8,128)(2,1)} %fusion.46) | data formatting | bytes 8388608
  73.4 3.2 %multiply_convert_fusion.3 = bf16[32,128,8,64]{1,0,3,2:T(8,128)(2,1)} fusion(bf16[32,128,8,64]{1,0,3,2:T(8,128)(2,1)S(1)} %bitcast.95, f32[32,128,8]{1,0,2:T(8,128)S(1)} %copy.22), kind=kLoop, calls=%fused_computation.24 | loop fusion | flops 6291456 | bytes 8519680 | tf_op jit(solution)/shard_map/convert_element_type | solution.py:56
  76.6 8.8 %collective-permute-done.3 = bf16[4096,128]{0,1:T(8,128)(2,1)S(1)} collective-permute-done((bf16[4096,128]{0,1:T(8,128)(2,1)S(1)}, bf16[4096,128]{0,1:T(8,128)(2,1)S(1)}, u32[]{:S(2)}, u32[]{:S(2)}) %collective-permute-start.3) | collective-permute-done | bytes 1048608 | tf_op jit(solution)/shard_map/ppermute | solution.py:21
  86.7 7.6 %fusion.16 = f32[32,8,64,128]{3,2,1,0:T(8,128)} fusion(bf16[32,128,128,1]{2,1,3,0:T(8,128)(2,1)S(1)} %bitcast.97, bf16[32,128,8,64]{1,0,3,2:T(8,128)(2,1)} %multiply_convert_fusion.3), kind=kOutput, calls=%fused_computation.33 | convolution fusion | flops 536870912 | bytes 13631488 | tf_op jit(solution)/shard_map/cshp,csn->chpn/dot_general | solution.py:59
  94.3 79.0 %while.13 = (s32[]{:T(128)}, f32[8,64,128]{2,1,0:T(8,128)S(1)}, f32[32,8,64,128]{3,2,1,0:T(8,128)}, f32[32,8]{1,0:T(8,128)}, f32[32,8,64,128]{3,2,1,0:T(8,128)}, /*index=5*/s32[]{:T(128)}, s32[]{:T(128)}) while((s32[]{:T(128)}, f32[8,64,128]{2,1,0:T(8,128)S(1)}, f32[32,8,64,128]{3,2,1,0:T(8,128)}, f32[32,8]{1,0:T(8,128)}, ...), condition=%wide.region_2.3_spmd.clone, body=%wide.region_1.2_spmd.clone.sunk | while | flops 262147 | bytes 1311424 | solution.py:66
  95.7 1.0 bitcast_add_fusion.4
  98.2 1.0 bitcast_add_fusion.4
  103.2 1.0 bitcast_add_fusion.4
  108.1 1.0 bitcast_add_fusion.4
  110.6 1.0 bitcast_add_fusion.4
  113.0 1.0 bitcast_add_fusion.4
  118.0 1.0 bitcast_add_fusion.4
  120.5 1.0 bitcast_add_fusion.4
  123.0 1.0 bitcast_add_fusion.4
  125.4 1.0 bitcast_add_fusion.4
  130.4 1.0 bitcast_add_fusion.4
  135.3 1.0 bitcast_add_fusion.4
  140.2 1.0 bitcast_add_fusion.4
  142.7 1.0 bitcast_add_fusion.4
  145.2 1.0 bitcast_add_fusion.4
  147.6 1.0 bitcast_add_fusion.4
  150.1 1.0 bitcast_add_fusion.4
  152.6 1.0 bitcast_add_fusion.4
  164.9 1.0 bitcast_add_fusion.4
  167.4 1.0 bitcast_add_fusion.4
  169.9 1.0 bitcast_add_fusion.4
  172.3 1.0 bitcast_add_fusion.4
  174.1 1.2 stack.2
  175.3 6.0 %all-to-all-start = ((bf16[8,1,8,64,128]{4,3,2,1,0:T(8,128)(2,1)}), bf16[8,1,8,64,128]{4,3,2,1,0:T(8,128)(2,1)S(1)}, u32[]{:S(2)}, u32[]{:S(2)}) async-start(bf16[8,1,8,64,128]{4,3,2,1,0:T(8,128)(2,1)} %stack.2), calls=%async_computation | async-start | bytes 2097152 | tf_op jit(solution)/shard_map/all_to_all | solution.py:80
  182.2 8.4 %fusion.36 = f32[32,128,8,64]{1,3,2,0:T(8,128)} fusion(bf16[32,128,128,1]{2,1,3,0:T(8,128)(2,1)S(1)} %bitcast.93, f32[32,8,64,128]{3,2,1,0:T(8,128)} %get-tuple-element.33), kind=kOutput, calls=%fused_computation.77 | convolution fusion | flops 3221225472 | bytes 17825792 | tf_op jit(solution)/shard_map/ctn,chpn->cthp/dot_general | solution.py:68
  190.6 10.7 %fusion.1 = f32[32,8,64,128]{3,2,1,0:T(8,128)} fusion(f32[32,8,128]{2,1,0:T(8,128)S(1)} %copy-done.9, f32[32,8,128]{2,1,0:T(8,128)S(1)} %reduce_window_sum.22, f32[32,128,128]{2,1,0:T(8,128)S(1)} %fusion.35, pred[128,128]{1,0:T(8,128)(4,1)S(1)} %copy-done.11, bf16[32,128,8,64]{1,0,3,2:T(8,128)(2,1)S(1)} %bitcast.96), kind=kOutput, calls=%fused_computation.7 | convolution fusion | flops 562036736 | bytes 14958592 | tf_op jit(solution)/shard_map/chts,cshp->cthp/dot_general | solution.py:53
  201.3 7.6 %all-to-all-done = bf16[8,1,8,64,128]{4,3,2,1,0:T(8,128)(2,1)S(1)} async-done(((bf16[8,1,8,64,128]{4,3,2,1,0:T(8,128)(2,1)}), bf16[8,1,8,64,128]{4,3,2,1,0:T(8,128)(2,1)S(1)}, u32[]{:S(2)}, u32[]{:S(2)}) %all-to-all-start) | async-done | bytes 1048608 | tf_op jit(solution)/shard_map/all_to_all | solution.py:80
  208.9 1.3 fusion.24
  210.3 8.3 %fusion.9 = f32[32,128,8,64]{1,3,2,0:T(8,128)S(1)} fusion(f32[32,8,64,128]{3,2,1,0:T(8,128)} %fusion.1, f32[32,128,8,64]{1,3,2,0:T(8,128)} %fusion.36, f32[32,128,8]{1,2,0:T(8,128)S(1)} %copy-done.7, f32[32,128,8]{1,2,0:T(8,128)S(1)} %copy-done.6, bf16[32,128,128,1]{2,1,3,0:T(8,128)(2,1)S(1)} %bitcast.94, f32[8,64,128,1]{2,1,0,3:T(8,128)S(1)} %bitcast.100), kind=kOutput, calls=%fused_computation.21 | convolution fusion | flops 3229614080 | bytes 26738688 | tf_op jit(solution)/shard_map/ctn,hpn->cthp/dot_general | solution.py:132
  218.6 8.0 %copy.27 = f32[32,128,8,64]{1,0,3,2:T(8,128)} copy(f32[32,128,8,64]{1,3,2,0:T(8,128)S(1)} %fusion.9) | data formatting | bytes 16777216 | tf_op jit(solution)/shard_map/add | solution.py:133
  226.7 14.2 %multiply_reduce_fusion = (f32[4096]{0:T(1024)S(1)}, f32[4096,512]{0,1:T(8,128)S(1)}) fusion(bf16[4096,512]{0,1:T(8,128)(2,1)S(1)} %copy-done.4, f32[512]{0:T(512)S(1)} %copy-done.13, f32[64,8,32,128]{3,2,1,0:T(8,128)} %bitcast.91, f32[4099,512]{0,1:T(8,128)S(1)} %bitcast.90, f32[512]{0:T(512)S(1)} %bitcast.110, f32[512]{0:T(512)S(1)} %bitcast.108, ...), kind=kLoop, calls=%fused_computation.23 | loop fusion | flops 48230400 | bytes 54552576 | tf_op jit(solution)/shard_map/reduce_sum | solution.py:138
  240.9 1.2 collective-permute-done.4
  242.6 3.2 %collective-permute-done.5 = f32[4096]{0:T(1024)S(1)} collective-permute-done((f32[4096]{0:T(1024)S(1)}, f32[4096]{0:T(1024)S(1)}, u32[]{:S(2)}, u32[]{:S(2)}) %collective-permute-start.5) | collective-permute-done | bytes 16416 | tf_op jit(solution)/shard_map/ppermute | solution.py:21
  245.9 3.3 %multiply_convert_fusion.2 = bf16[4096,512]{0,1:T(8,128)(2,1)} fusion(f32[4096,512]{0,1:T(8,128)S(1)} %get-tuple-element.69, f32[512]{0:T(512)S(1)} %copy-done.15, f32[4096]{0:T(1024)S(1)} %add_rsqrt_fusion), kind=kLoop, calls=%fused_computation.22 | loop fusion | flops 6291456 | bytes 12601344 | tf_op jit(solution)/shard_map/convert_element_type | solution.py:143
  249.2 6.4 %copy.29 = bf16[4096,512]{1,0:T(8,128)(2,1)} copy(bf16[4096,512]{0,1:T(8,128)(2,1)} %multiply_convert_fusion.2) | data formatting | bytes 8388608 | tf_op jit(solution)/shard_map/convert_element_type | solution.py:143
  (169 shorter events, 70.5 us)
Async XLA Ops:
  0.0 27.5 %copy-start.19 = (u32[256]{0:T(256)S(1)}, u32[256]{0:T(256)}, u32[]{:S(2)}) copy-start(u32[256]{0:T(256)} %constant.53) | copy-start | bytes 3076
  0.0 16.0 %copy-start.18 = (f32[8]{0:T(128)S(1)}, f32[8]{0:T(128)}, u32[]{:S(2)}) copy-start(f32[8]{0:T(128)} %param.17) | copy-start | bytes 100
  0.0 16.0 %copy-start.8 = (f32[4096,8]{0,1:T(8,128)S(1)}, f32[4096,8]{0,1:T(8,128)}, u32[]{:S(2)}) copy-start(f32[4096,8]{0,1:T(8,128)} %param.15) | copy-start | bytes 393220
  0.0 16.0 %copy-start.14 = (f32[8]{0:T(128)S(1)}, f32[8]{0:T(128)}, u32[]{:S(2)}) copy-start(f32[8]{0:T(128)} %param.16) | copy-start | bytes 100
  0.0 27.2 %copy-start.16 = (bf16[4,64]{1,0:T(4,128)(2,1)S(1)}, bf16[4,64]{1,0:T(4,128)(2,1)}, u32[]{:S(2)}) copy-start(bf16[4,64]{1,0:T(4,128)(2,1)} %param.20) | copy-start | bytes 1540
  0.0 27.2 %copy-start.12 = (bf16[4,512]{1,0:T(4,128)(2,1)S(1)}, bf16[4,512]{1,0:T(4,128)(2,1)}, u32[]{:S(2)}) copy-start(bf16[4,512]{1,0:T(4,128)(2,1)} %param.19) | copy-start | bytes 12292
  0.9 54.6 %collective-permute-start.1 = (bf16[3,64]{0,1:T(8,128)(2,1)S(1)}, bf16[3,64]{0,1:T(8,128)(2,1)S(1)}, u32[]{:S(2)}, u32[]{:S(2)}) collective-permute-start(bf16[3,64]{0,1:T(8,128)(2,1)S(1)} %slice.73), channel_id=1, source_target_pairs={{0,32},{32,64},{64,96},{96,128},{128,160},{160,192},{192,224},{1,3... | collective-permute-start | bytes 1160 | tf_op jit(solution)/shard_map/ppermute | solution.py:15
  5.6 51.2 %collective-permute-start = (bf16[3,512]{0,1:T(8,128)(2,1)S(1)}, bf16[3,512]{0,1:T(8,128)(2,1)S(1)}, u32[]{:S(2)}, u32[]{:S(2)}) collective-permute-start(bf16[3,512]{0,1:T(8,128)(2,1)S(1)} %copy.15), channel_id=1, source_target_pairs={{0,32},{32,64},{64,96},{96,128},{128,160},{160,192},{192,224},{1,3... | collective-permute-start | bytes 9224 | tf_op jit(solution)/shard_map/ppermute | solution.py:15
  9.5 45.4 %copy-start.17 = (f32[8]{0:T(128)S(1)}, f32[8]{0:T(128)}, u32[]{:S(2)}) copy-start(f32[8]{0:T(128)} %param.18) | copy-start | bytes 100
  9.5 46.0 %copy-start.5 = (bf16[4096,64]{0,1:T(8,128)(2,1)S(1)}, bf16[4096,64]{0,1:T(8,128)(2,1)}, u32[]{:S(2)}) copy-start(bf16[4096,64]{0,1:T(8,128)(2,1)} %param.14) | copy-start | bytes 1572868
  55.5 2.2 copy-start.1
  56.7 3.5 %collective-permute-start.2 = (bf16[4096,64]{0,1:T(8,128)(2,1)S(1)}, bf16[4096,64]{0,1:T(8,128)(2,1)S(1)}, u32[]{:S(2)}, u32[]{:S(2)}) collective-permute-start(bf16[4096,64]{0,1:T(8,128)(2,1)S(1)} %multiply_convert_fusion.5), channel_id=1, source_target_pairs={{0,1},{1,0},{2,3},{3,2},{4,5},{5,4},{6,7},{7,6},{8,9},{9,8},{10,11... | collective-permute-start | bytes 1572872 | tf_op jit(solution)/shard_map/ppermute | solution.py:21
  60.2 9.7 %copy-start = (f32[4099,512]{0,1:T(8,128)}, f32[4099,512]{0,1:T(8,128)S(1)}, u32[]{:S(2)}) copy-start(f32[4099,512]{0,1:T(8,128)S(1)} %maximum_convert_fusion) | copy-start | bytes 25184260
  60.5 24.9 %collective-permute-start.3 = (bf16[4096,128]{0,1:T(8,128)(2,1)S(1)}, bf16[4096,128]{0,1:T(8,128)(2,1)S(1)}, u32[]{:S(2)}, u32[]{:S(2)}) collective-permute-start(bf16[4096,128]{0,1:T(8,128)(2,1)S(1)} %maximum_select_fusion.1), channel_id=1, source_target_pairs={{0,2},{1,3},{2,0},{3,1},{4,6},{5,7},{6,4},{7,5},{8,10},{9,11},{10,... | collective-permute-start | bytes 3145736 | tf_op jit(solution)/shard_map/ppermute | solution.py:21
  73.4 12.7 %copy-start.2 = (bf16[64,8,32,128]{3,2,1,0:T(8,128)(2,1)}, bf16[64,8,32,128]{3,2,1,0:T(8,128)(2,1)S(1)}, u32[]{:S(2)}) copy-start(bf16[64,8,32,128]{3,2,1,0:T(8,128)(2,1)S(1)} %copy.37) | copy-start | bytes 12582916
  175.3 33.6 %all-to-all-start = ((bf16[8,1,8,64,128]{4,3,2,1,0:T(8,128)(2,1)}), bf16[8,1,8,64,128]{4,3,2,1,0:T(8,128)(2,1)S(1)}, u32[]{:S(2)}, u32[]{:S(2)}) async-start(bf16[8,1,8,64,128]{4,3,2,1,0:T(8,128)(2,1)} %stack.2), calls=%async_computation | async-start | bytes 2097152 | tf_op jit(solution)/shard_map/all_to_all | solution.py:80
  182.2 8.4 %copy-start.3 = (bf16[64,8,32,128]{3,2,1,0:T(8,128)(2,1)S(1)}, bf16[64,8,32,128]{3,2,1,0:T(8,128)(2,1)}, u32[]{:S(2)}) copy-start(bf16[64,8,32,128]{3,2,1,0:T(8,128)(2,1)} %copy-done.2) | copy-start | bytes 12582916
  182.2 8.4 %copy-start.9 = (f32[32,8,128]{2,1,0:T(8,128)S(1)}, f32[32,8,128]{2,1,0:T(8,128)}, u32[]{:S(2)}) copy-start(f32[32,8,128]{2,1,0:T(8,128)} %get-tuple-element.73) | copy-start | bytes 393220
  182.2 8.4 %copy-start.11 = (pred[128,128]{1,0:T(8,128)(4,1)S(1)}, pred[128,128]{1,0:T(8,128)(4,1)}, u32[]{:S(2)}) copy-start(pred[128,128]{1,0:T(8,128)(4,1)} %iota_compare_fusion) | copy-start | bytes 49156
  190.6 18.3 %copy-start.10 = (f32[8,8,1,1]{0,2,3,1:T(1,128)S(1)}, f32[8,8,1,1]{0,2,3,1:T(1,128)}, u32[]{:S(2)}) copy-start(f32[8,8,1,1]{0,2,3,1:T(1,128)} %copy.32) | copy-start | bytes 772
  190.6 19.6 %copy-start.6 = (f32[32,128,8]{1,2,0:T(8,128)S(1)}, f32[32,128,8]{1,2,0:T(8,128)}, u32[]{:S(2)}) copy-start(f32[32,128,8]{1,2,0:T(8,128)} %get-tuple-element.76) | copy-start | bytes 393220
  190.6 19.6 %copy-start.7 = (f32[32,128,8]{1,2,0:T(8,128)S(1)}, f32[32,128,8]{1,2,0:T(8,128)}, u32[]{:S(2)}) copy-start(f32[32,128,8]{1,2,0:T(8,128)} %get-tuple-element.77) | copy-start | bytes 393220
  210.2 16.4 %slice-start = ((s8[8650752]{0:T(1024)(128)(4,1)}), s8[4194304]{0:T(1024)(128)(4,1)S(1)}, s32[]{:S(2)}) async-start(s8[8650752]{0:T(1024)(128)(4,1)} %bitcast.89), calls=%async_computation.1 | async-start | bytes 8388608
  210.3 16.4 %slice-start.1 = ((s8[8650752]{0:T(1024)(128)(4,1)}), s8[4194304]{0:T(1024)(128)(4,1)S(1)}, s32[]{:S(2)}) async-start(s8[8650752]{0:T(1024)(128)(4,1)} %bitcast.89), calls=%async_computation.2 | async-start | bytes 8388608
  218.6 8.1 %slice-start.2 = ((s8[8650752]{0:T(1024)(128)(4,1)}), s8[262144]{0:T(1024)(128)(4,1)S(1)}, s32[]{:S(2)}) async-start(s8[8650752]{0:T(1024)(128)(4,1)} %bitcast.89), calls=%async_computation.3 | async-start | bytes 524288
  218.6 8.0 %copy-start.4 = (bf16[4096,512]{0,1:T(8,128)(2,1)S(1)}, bf16[4096,512]{0,1:T(8,128)(2,1)}, u32[]{:S(2)}) copy-start(bf16[4096,512]{0,1:T(8,128)(2,1)} %copy.28) | copy-start | bytes 12582916
  218.6 8.0 %copy-start.13 = (f32[512]{0:T(512)S(1)}, f32[512]{0:T(512)}, u32[]{:S(2)}) copy-start(f32[512]{0:T(512)} %mul.228) | copy-start | bytes 6148
  226.7 19.2 %copy-start.15 = (f32[512]{0:T(512)S(1)}, f32[512]{0:T(512)}, u32[]{:S(2)}) copy-start(f32[512]{0:T(512)} %param.21) | copy-start | bytes 6148
  240.8 1.3 collective-permute-start.4
  242.1 3.7 %collective-permute-start.5 = (f32[4096]{0:T(1024)S(1)}, f32[4096]{0:T(1024)S(1)}, u32[]{:S(2)}, u32[]{:S(2)}) collective-permute-start(f32[4096]{0:T(1024)S(1)} %add.99), channel_id=1, source_target_pairs={{0,2},{1,3},{2,0},{3,1},{4,6},{5,7},{6,4},{7,5},{8,10},{9,11},{10,... | collective-permute-start | bytes 49160 | tf_op jit(solution)/shard_map/ppermute | solution.py:21
